TPU v7x, 128 devices: a whole 4x4x4 slice. The times are simulated.
128 devices in a mesh: dp: 32 (over x, y_lo, z), gz: 4 (over y_hi, core).
Axes of the slice: x: 4, y: 4 (y_hi: 2, y_lo: 2; y = y_hi * 2 + y_lo), z: 4, core: 2. Of those that a mesh axis runs over, the one named last changes fastest.
Arguments:
- field: bfloat16 [32, 16, 96, 9216], P('dp', None, 'gz'), may hold values from -6 to 6
- cotangent: bfloat16 [32, 16, 96, 9216], P('dp', None, 'gz'), may hold values from -36 to 36, as said below
- spec_weight: float32 [16, 16, 16, 256], P('gz'), may hold values from -1.5 to 1.5
- point_weight: bfloat16 [16, 16], replicated, may hold values from -1.5 to 1.5
- bias: float32 [16], replicated, may hold values from -3 to 3
Outputs:
- field_grad: bfloat16 [32, 16, 96, 9216], P('dp', None, 'gz')
- spectral_grad: float32 [16, 16, 16, 256], P('gz')
- point_grad: float32 [16, 16], replicated
- bias_grad: float32 [16], replicated
Inputs may be any that keep to these rules, and one draw needn't show every extreme that they name: `cotangent`: the gradient of the loss with respect to the layer's output.
All inputs are finite; a program needn't handle non-finite values.
Results may differ from a plain program's by a relative error of at most 0.007.
Values sent between devices are 32-bit elements; how exact they have to be, the bound alone decides.
No kernel may reach another device: no remote copies, remote signals or barrier semaphores. Data moves between devices by JAX's collectives and lax.ppermute only.
A program may use at most 192 MiB of HBM per device.

v0:
```python
import math
import jax
import jax.numpy as jnp
from jax import lax
from jax.sharding import PartitionSpec as P

N = 96
M = 16
root_half = 0.7071067811865476
density_norm = 0.3989422804014327


def basis_table(count_modes, length):
    mode_index = jnp.arange(count_modes, dtype=jnp.int32)
    half_count = count_modes // 2
    frequency = jnp.where(mode_index < half_count, mode_index, mode_index - half_count + 1)
    position = jnp.arange(length, dtype=jnp.int32)
    turns = frequency[:, None] * position[None, :] % length
    angle = turns.astype(jnp.float32) * (2.0 * math.pi / length)
    return jnp.where((mode_index < half_count)[:, None], jnp.cos(angle), jnp.sin(angle))


def kron_table(basis):
    outer = basis[:, None, :, None] * basis[None, :, None, :]
    return outer.reshape(M * M, N * N)


def gelu_slope(values):
    cumulative = 0.5 * (1.0 + lax.erf(values * root_half))
    return cumulative + values * jnp.exp(-0.5 * values * values) * density_norm


def shards(field, cotangent, spec_weight, point_weight, bias):
    highest = lax.Precision.HIGHEST
    samples_dev, channels, slab_rows, plane_cells = field.shape
    scale_fwd = (2.0 / N) ** 1.5
    scale_inv = (2.0 / M) ** 1.5
    basis = basis_table(M, N)
    kron = kron_table(basis)
    row_basis = lax.dynamic_slice_in_dim(basis, lax.axis_index("gz") * slab_rows, slab_rows, 1)
    contract_cells = (((1,), (1,)), ((), ()))

    def to_modes(values):
        flattened = values.reshape(samples_dev * channels * slab_rows, plane_cells).astype(
            jnp.float32
        )
        return lax.dot_general(flattened, kron, contract_cells, precision=highest).reshape(
            samples_dev, channels, slab_rows, M * M
        )

    def add_inverse(piece):
        piece_rows = piece.shape[0]
        inner = jnp.dot(
            piece.reshape(piece_rows * samples_dev * channels, M * M), kron, precision=highest
        )
        inner = inner.reshape(piece_rows, samples_dev, channels, plane_cells)
        return jnp.einsum("ax,asoz->soxz", row_basis, inner, precision=highest)

    line_modes = to_modes(field)
    rows_part = row_basis
    coefficients = lax.psum_scatter(
        scale_fwd * jnp.einsum("ax,scxp->ascp", rows_part, line_modes, precision=highest),
        "gz",
        scatter_dimension=0,
        tiled=True,
    )
    mixed_modes = jnp.einsum("asip,aiop->asop", coefficients, spec_weight, precision=highest)
    spectral = scale_inv * add_inverse(lax.all_gather(mixed_modes, "gz", axis=0, tiled=True))
    pre_act = (
        spectral
        + jnp.einsum("sixz,io->soxz", field, point_weight, preferred_element_type=jnp.float32)
        + bias[None, :, None, None]
    )
    grad_pre = (cotangent.astype(jnp.float32) * gelu_slope(pre_act)).astype(jnp.bfloat16)
    grad_line = to_modes(grad_pre)
    rows_part = row_basis
    grad_modes = lax.psum_scatter(
        scale_inv * jnp.einsum("ax,soxp->asop", rows_part, grad_line, precision=highest),
        "gz",
        scatter_dimension=0,
        tiled=True,
    )
    back_modes = jnp.einsum("aiop,asop->asip", spec_weight, grad_modes, precision=highest)
    field_spec = scale_fwd * add_inverse(lax.all_gather(back_modes, "gz", axis=0, tiled=True))
    field_grad = (
        field_spec
        + jnp.einsum("soxz,io->sixz", grad_pre, point_weight, preferred_element_type=jnp.float32)
    ).astype(jnp.bfloat16)
    local_point = jnp.einsum("sixz,soxz->io", field, grad_pre, preferred_element_type=jnp.float32)
    local_bias = jnp.sum(grad_pre, axis=(0, 2, 3), dtype=jnp.float32)
    total_point, total_bias = lax.psum((local_point, local_bias), ("dp", "gz"))
    local_spec = jnp.einsum("asip,asop->aiop", coefficients, grad_modes, precision=highest)
    grad_spec = lax.psum(local_spec, "dp")
    all_samples = samples_dev * lax.axis_size("dp")
    cell_norm = math.sqrt(all_samples * N * N * N)
    return (
        field_grad,
        grad_spec / math.sqrt(all_samples * N),
        total_point / cell_norm,
        total_bias / cell_norm,
    )


def solution(mesh):
    return jax.shard_map(
        shards,
        mesh=mesh,
        in_specs=(
            P("dp", None, "gz", None),
            P("dp", None, "gz", None),
            P("gz", None, None, None),
            P(),
            P(),
        ),
        out_specs=(P("dp", None, "gz", None), P("gz", None, None, None), P(), P()),
        check_vma=False,
    )
```

profile of v0, /device:TPU:0, one launch (start us, length us, event | category | flops | bytes accessed | tf_op | source)
XLA Modules:
  0.0 559.2 jit_solution(4819427986787261615)
XLA Ops:
  7.2 0.0 copy-start
  7.2 0.0 reduce-scatter.3.cloned.1.call-start
  7.3 0.1 sine_select_fusion
  7.4 6.2 %broadcast_multiply_fusion = f32[16,16,96,96]{3,2,1,0:T(8,128)} fusion(f32[16,96]{1,0:T(8,128)S(1)} %sine_select_fusion), kind=kLoop, calls=%fused_computation.12 | loop fusion | flops 2359296 | bytes 9443328 | tf_op jit(solution)/shard_map/mul | solution.py:24
  13.6 12.8 %mul.213 = f32[256,9216]{1,0:T(8,128)} reshape(f32[16,16,96,96]{3,2,1,0:T(8,128)} %broadcast_multiply_fusion) | data formatting | bytes 18874368 | tf_op jit(solution)/shard_map/mul | solution.py:24
  26.4 11.1 %convolution_bitcast_fusion = f32[384,256]{0,1:T(8,128)S(1)} fusion(f32[256,9216]{1,0:T(8,128)} %mul.213, bf16[384,9216]{1,0:T(8,128)(2,1)} %bitcast.98), kind=kOutput, calls=%fused_computation.20 | convolution fusion | flops 10871635968 | bytes 16908288 | tf_op jit(solution)/shard_map/dot_general | solution.py:47
  37.5 0.2 copy.31
  37.7 0.4 fusion.16
  38.1 0.9 copy.32
  39.0 0.0 reduce-scatter.3.cloned.1.call-update
  39.0 0.0 reduce-scatter.5.cloned.1.call-start
  39.0 12.9 %reshape.211 = f32[256,9216,1]{1,0,2:T(8,128)} reshape(f32[16,16,96,96]{3,2,1,0:T(8,128)} %broadcast_multiply_fusion) | data formatting | bytes 18874368 | tf_op jit(solution)/shard_map/mul | solution.py:24
  51.9 0.0 copy-done
  51.9 11.7 %fusion.13 = f32[16,24,9216]{2,0,1:T(8,128)} fusion(bf16[16,24,9216]{2,1,0:T(8,128)(2,1)} %bitcast.99, bf16[16,16]{1,0:T(8,128)(2,1)S(1)} %copy-done), kind=kOutput, calls=%fused_computation.18 | convolution fusion | flops 113246208 | bytes 21234176 | tf_op jit(solution)/shard_map/sixz,io->soxz/dot_general | solution.py:71
  63.6 5.0 reduce-scatter.3.cloned.1.call-done
  68.6 0.0 copy-done.1
  68.6 1.1 multiply_reduce_fusion.1
  69.8 7.4 %all_gather.6 = f32[16,1,16,256]{3,2,1,0:T(8,128)S(1)} all-gather(f32[4,1,16,256]{3,2,1,0:T(8,128)S(1)} %bitcast.109), channel_id=1, replica_groups=mesh['dp'=32,'gz'=4] {'gz'}, dimensions={0}, use_global_device_ids=true | all-gather | bytes 327680 | tf_op jit(solution)/shard_map/all_gather | solution.py:68
  77.2 12.2 %fusion.24 = f32[16,16,9216]{2,0,1:T(8,128)S(1)} fusion(f32[256,9216,1]{1,0,2:T(8,128)} %reshape.211, f32[16,1,16,256]{3,2,1,0:T(8,128)S(1)} %all_gather.6), kind=kOutput, calls=%fused_computation.32 | convolution fusion | flops 7247757312 | bytes 19136512 | tf_op jit(solution)/shard_map/dot_general | solution.py:53
  89.4 0.0 slice-done.5
  89.4 0.0 slice-done.6
  89.4 0.0 copy-done.3
  89.4 0.0 slice-start.1
  89.4 0.0 slice-start.2
  89.4 25.9 %convert_reduce_fusion = (f32[16]{0:T(128)S(1)}, bf16[1,16,24,9216]{3,2,1,0:T(8,128)(2,1)}) fusion(f32[16]{0:T(128)S(1)} %copy-done.3, f32[16,24,9216]{2,0,1:T(8,128)} %fusion.13, f32[16,16,9216]{2,0,1:T(8,128)S(1)} %fusion.24, f32[16,96]{1,0:T(8,128)S(1)} %sine_select_fusion, s32[]{:T(128)S(6)} %select_n.65, bf16[1,16,24,9216]{3,2,1,0:T(8,128)(2,1)S(1)} %bitcast.112), kind=kOutput, calls=%fused_computation.11 | convolution fusion | flops 736100352 | bytes 37755012 | tf_op jit(solution)/shard_map/ax,asoz->soxz/dot_general | solution.py:57
  115.4 0.0 slice-done
  115.4 0.0 slice-done.1
  115.4 0.0 slice-start.4
  115.4 13.4 %fusion.47 = f32[16,24,256]{2,1,0:T(8,128)S(1)} fusion(f32[256,9216,1]{1,0,2:T(8,128)S(1)} %bitcast.97, bf16[1,16,24,9216]{3,2,1,0:T(8,128)(2,1)} %get-tuple-element.21), kind=kOutput, calls=%fused_computation.62 | convolution fusion | flops 10871635968 | bytes 16908288 | tf_op jit(solution)/shard_map/dot_general | solution.py:47
  128.8 0.0 slice-done.3
  128.8 0.0 slice-done.4
  128.9 17.8 %fusion.17 = f32[16,16]{0,1:T(8,128)S(1)} fusion(bf16[16,24,9216]{2,1,0:T(8,128)(2,1)S(1)} %bitcast.102, bf16[16,24,9216]{2,1,0:T(8,128)(2,1)} %bitcast.103), kind=kOutput, calls=%fused_computation.25 | convolution fusion | flops 113246208 | bytes 14156800 | tf_op jit(solution)/shard_map/sixz,soxz->io/dot_general | solution.py:89
  146.7 65.4 %all-reduce = (f32[16,16]{0,1:T(8,128)S(1)}, f32[16]{0:T(128)S(1)}) all-reduce(f32[16,16]{0,1:T(8,128)S(1)} %fusion.17, f32[16]{0:T(128)S(1)} %get-tuple-element.20), channel_id=1, replica_groups=mesh['dp'=32,'gz'=4] {'dp','gz'}, use_global_device_ids=true, to_apply=%region_3.4 | all-reduce | flops 272 | bytes 2176 | tf_op jit(solution)/shard_map/psum | solution.py:91
  212.2 0.7 copy.43
  212.8 0.5 broadcast_multiply_fusion.3
  213.4 0.4 fusion.15
  213.8 0.9 copy.37
  214.6 0.0 reduce-scatter.5.cloned.1.call-update
  214.7 0.0 all-reduce.3.cloned.1.call-start
  214.7 16.0 %fusion.10 = f32[24,9216,16]{1,2,0:T(8,128)} fusion(bf16[16,24,9216]{2,1,0:T(8,128)(2,1)} %bitcast.104, bf16[16,16]{1,0:T(8,128)(2,1)S(1)} %copy-done), kind=kOutput, calls=%fused_computation.15 | convolution fusion | flops 113246208 | bytes 21234176 | tf_op jit(solution)/shard_map/soxz,io->sixz/dot_general | solution.py:87
  230.7 8.1 %reduce-scatter.5.cloned.1.call-done = f32[4,1,16,256]{3,2,1,0:T(8,128)} async-done(((f32[16,1,16,256]{3,2,1,0:T(8,128)}), f32[4,1,16,256]{3,2,1,0:T(8,128)}) %reduce-scatter.5.cloned.1.call-update) | async-done | bytes 65552 | tf_op jit(solution)/shard_map/reduce_scatter | solution.py:77
  238.8 2.1 multiply_bitcast_fusion
  240.8 0.0 all-reduce.3.cloned.1.call-update
  240.9 7.3 %all_gather.7 = f32[16,1,16,256]{3,2,1,0:T(8,128)S(1)} all-gather(f32[4,1,16,256]{3,2,1,0:T(8,128)S(1)} %bitcast.108), channel_id=1, replica_groups=mesh['dp'=32,'gz'=4] {'gz'}, dimensions={0}, use_global_device_ids=true | all-gather | bytes 327680 | tf_op jit(solution)/shard_map/all_gather | solution.py:84
  248.2 12.2 %fusion.22 = f32[16,16,9216]{2,0,1:T(8,128)S(1)} fusion(f32[256,9216,1]{1,0,2:T(8,128)} %reshape.211, f32[16,1,16,256]{3,2,1,0:T(8,128)S(1)} %all_gather.7), kind=kOutput, calls=%fused_computation.30 | convolution fusion | flops 7247757312 | bytes 19136512 | tf_op jit(solution)/shard_map/dot_general | solution.py:53
  260.4 25.8 %fusion.6 = bf16[1,16,24,9216]{3,2,1,0:T(8,128)(2,1)} fusion(f32[24,9216,16]{1,2,0:T(8,128)} %fusion.10, f32[16,16,9216]{2,0,1:T(8,128)S(1)} %fusion.22, f32[16,96]{1,0:T(8,128)S(1)} %sine_select_fusion, s32[]{:T(128)S(6)} %select_n.65), kind=kOutput, calls=%fused_computation.8 | convolution fusion | flops 690094080 | bytes 30676996 | tf_op jit(solution)/shard_map/ax,asoz->soxz/dot_general | solution.py:57
  286.2 263.8 %all-reduce.3.cloned.1.call-done = f32[4,16,16,256]{3,2,1,0:T(8,128)} async-done(((f32[4,16,16,256]{3,2,1,0:T(8,128)}), f32[4,16,16,256]{3,2,1,0:T(8,128)}) %all-reduce.3.cloned.1.call-update) | async-done | bytes 1048592 | tf_op jit(solution)/shard_map/psum | solution.py:93
  550.0 2.3 broadcast_multiply_fusion.1
  (15 shorter events, 0.0 us)
Async XLA Ops:
  7.2 44.8 %copy-start = (bf16[16,16]{1,0:T(8,128)(2,1)S(1)}, bf16[16,16]{1,0:T(8,128)(2,1)}, u32[]{:S(2)}) copy-start(bf16[16,16]{1,0:T(8,128)(2,1)} %param.8) | copy-start | bytes 1540
  7.2 61.4 %reduce-scatter.3.cloned.1.call-start = ((), (), s32[]{:S(2)}) async-start(), calls=%async_computation.2 | async-start | bytes 327680 | tf_op jit(solution)/shard_map/reduce_scatter | solution.py:61
  39.0 199.8 %reduce-scatter.5.cloned.1.call-start = ((), (), s32[]{:S(2)}) async-start(), calls=%async_computation.3 | async-start | bytes 327680 | tf_op jit(solution)/shard_map/reduce_scatter | solution.py:77
  51.9 16.7 %copy-start.1 = (f32[4,16,16,256]{3,2,1,0:T(8,128)S(1)}, f32[4,16,16,256]{3,2,1,0:T(8,128)}, u32[]{:S(2)}) copy-start(f32[4,16,16,256]{3,2,1,0:T(8,128)} %param.7) | copy-start | bytes 3145732
  68.6 20.8 %slice-start.5 = ((s8[7077888]{0:T(1024)(128)(4,1)}), s8[4194304]{0:T(1024)(128)(4,1)S(1)}, s32[]{:S(2)}) async-start(s8[7077888]{0:T(1024)(128)(4,1)} %bitcast.111), calls=%async_computation.10 | async-start | bytes 8388608
  77.2 12.2 %slice-start.6 = ((s8[7077888]{0:T(1024)(128)(4,1)}), s8[2883584]{0:T(1024)(128)(4,1)S(1)}, s32[]{:S(2)}) async-start(s8[7077888]{0:T(1024)(128)(4,1)} %bitcast.111), calls=%async_computation.11 | async-start | bytes 5767168
  77.2 12.2 %copy-start.3 = (f32[16]{0:T(128)S(1)}, f32[16]{0:T(128)}, u32[]{:S(2)}) copy-start(f32[16]{0:T(128)} %param.9) | copy-start | bytes 196
  77.2 38.2 %slice-start = ((s8[9437184]{0:T(1024)(128)(4,1)}), s8[4194304]{0:T(1024)(128)(4,1)S(1)}, s32[]{:S(2)}) async-start(s8[9437184]{0:T(1024)(128)(4,1)} %bitcast.96), calls=%async_computation.5 | async-start | bytes 8388608
  89.4 26.0 %slice-start.1 = ((s8[9437184]{0:T(1024)(128)(4,1)}), s8[4194304]{0:T(1024)(128)(4,1)S(1)}, s32[]{:S(2)}) async-start(s8[9437184]{0:T(1024)(128)(4,1)} %bitcast.96), calls=%async_computation.6 | async-start | bytes 8388608
  89.4 26.0 %slice-start.2 = ((s8[9437184]{0:T(1024)(128)(4,1)}), s8[1048576]{0:T(1024)(128)(4,1)S(1)}, s32[]{:S(2)}) async-start(s8[9437184]{0:T(1024)(128)(4,1)} %bitcast.96), calls=%async_computation.7 | async-start | bytes 2097152
  115.4 13.5 %slice-start.3 = ((s8[7077888]{0:T(1024)(128)(4,1)}), s8[4194304]{0:T(1024)(128)(4,1)S(1)}, s32[]{:S(2)}) async-start(s8[7077888]{0:T(1024)(128)(4,1)} %bitcast.100), calls=%async_computation.8 | async-start | bytes 8388608
  115.4 13.4 %slice-start.4 = ((s8[7077888]{0:T(1024)(128)(4,1)}), s8[2883584]{0:T(1024)(128)(4,1)S(1)}, s32[]{:S(2)}) async-start(s8[7077888]{0:T(1024)(128)(4,1)} %bitcast.100), calls=%async_computation.9 | async-start | bytes 5767168
  214.7 24.1 %copy-start.2 = (f32[4,1,16,256]{3,2,1,0:T(8,128)S(1)}, f32[4,1,16,256]{3,2,1,0:T(8,128)}, u32[]{:S(2)}) copy-start(f32[4,1,16,256]{3,2,1,0:T(8,128)} %reduce-scatter.3.cloned.1.call-done) | copy-start | bytes 196612
  214.7 335.3 %all-reduce.3.cloned.1.call-start = ((), (), s32[]{:S(2)}) async-start(), calls=%async_computation.4 | async-start | bytes 2097152 | tf_op jit(solution)/shard_map/psum | solution.py:93
Sparse Core Ops, SparseCore 0:
  39.1 29.4 reduce-scatter.2
  214.8 23.9 reduce-scatter.4
  241.8 308.1 all-reduce.2
where the time goes:
time: 568 us; the launch traced here: 559 us
  waiting for transfers between devices  277 us (49%)
  matrix products  147 us (26%)
  blocking collectives  80.2 us (14%)
  local copies, waits for them, and re-layouts  28.3 us (5%)
  between operations  14.3 us (3%)
  other arithmetic  12.4 us (2%)
    psum x1, waiting for transfers between devices, shards(): grad_spec = lax.psum(local_spec, 'dp')  264 us
    psum x1, blocking collectives, shards(): total_point, total_bias = lax.psum((local_point, local_bias), ('dp', 'gz'))  65.4 us
    dot_general x2, matrix products, add_inverse(): return jnp.einsum('ax,asoz->soxz', row_basis, inner, precision=highest)  51.8 us
    mul x2, local copies, waits for them, and re-layouts, kron_table(): outer = basis[:, None, :, None] * basis[None, :, None, :]  25.7 us
    dot_general x2, matrix products, to_modes(): lax.dot_general(flattened, kron, contract_cells, precision=highest)  24.5 us
    dot_general x2, matrix products, add_inverse(): jnp.dot(piece.reshape(piece_rows * samples_dev * channels, M * M), kron,...  24.4 us
    dot_general x1, matrix products, shards(): jnp.einsum('sixz,soxz->io', field, grad_pre, preferred_element_type=jnp.f...  17.8 us
    dot_general x1, matrix products, shards(): jnp.einsum('soxz,io->sixz', grad_pre, point_weight, preferred_element_typ...  16 us
  transfers between devices with their start and end apart: 3, of which 3 were waited for; matrix products, arithmetic and copies ran while one was open for 14% of the time, Pallas kernels for 0%

commit v1 on v0

--- a/solution.py
+++ b/solution.py
@@ -88,7 +88,7 @@
     ).astype(jnp.bfloat16)
     local_point = jnp.einsum("sixz,soxz->io", field, grad_pre, preferred_element_type=jnp.float32)
     local_bias = jnp.sum(grad_pre, axis=(0, 2, 3), dtype=jnp.float32)
-    total_point, total_bias = lax.psum((local_point, local_bias), ("dp", "gz"))
+    total_point, total_bias = lax.psum(lax.psum((local_point, local_bias), "dp"), "gz")
     local_spec = jnp.einsum("asip,asop->aiop", coefficients, grad_modes, precision=highest)
     grad_spec = lax.psum(local_spec, "dp")
     all_samples = samples_dev * lax.axis_size("dp")

time: 568 us -> 592 us (1.042)
  blocking collectives: 80.2 us -> 106 us
    psum x1 -> x2, blocking collectives: 65.4 us -> 91.3 us  [the longest x1 83.9 us: shards(): lax.psum((local_point, local_bias), 'dp')]
  transfers between devices with their start and end apart: 3 -> 3, of which waited for: 3 -> 3; matrix products, arithmetic and copies ran while one was open for 14% -> 13% of each run, Pallas kernels for 0% -> 0%
where the time goes in v1:
time: 592 us; the launch traced here: 583 us
  waiting for transfers between devices  275 us (46%)
  matrix products  147 us (25%)
  blocking collectives  106 us (18%)
  local copies, waits for them, and re-layouts  28.3 us (5%)
  between operations  14.4 us (2%)
  other arithmetic  12.4 us (2%)
    psum x1, waiting for transfers between devices, shards(): grad_spec = lax.psum(local_spec, 'dp')  264 us
    psum x1, blocking collectives, shards(): lax.psum((local_point, local_bias), 'dp')  83.9 us
    dot_general x2, matrix products, add_inverse(): return jnp.einsum('ax,asoz->soxz', row_basis, inner, precision=highest)  51.8 us
    mul x2, local copies, waits for them, and re-layouts, kron_table(): outer = basis[:, None, :, None] * basis[None, :, None, :]  25.7 us
    dot_general x2, matrix products, to_modes(): lax.dot_general(flattened, kron, contract_cells, precision=highest)  24.5 us
    dot_general x2, matrix products, add_inverse(): jnp.dot(piece.reshape(piece_rows * samples_dev * channels, M * M), kron,...  24.4 us
    dot_general x1, matrix products, shards(): jnp.einsum('sixz,soxz->io', field, grad_pre, preferred_element_type=jnp.f...  17.8 us
    dot_general x1, matrix products, shards(): jnp.einsum('soxz,io->sixz', grad_pre, point_weight, preferred_element_typ...  16 us
  transfers between devices with their start and end apart: 3, of which 3 were waited for; matrix products, arithmetic and copies ran while one was open for 13% of the time, Pallas kernels for 0%

profile of v1, /device:TPU:0, one launch (start us, length us, event | category | flops | bytes accessed | tf_op | source)
XLA Modules:
  0.0 583.4 jit_solution(17319083025714063063)
XLA Ops:
  7.2 0.0 copy-start
  7.2 0.0 reduce-scatter.3.cloned.1.call-start
  7.3 0.1 sine_select_fusion
  7.4 6.2 %broadcast_multiply_fusion = f32[16,16,96,96]{3,2,1,0:T(8,128)} fusion(f32[16,96]{1,0:T(8,128)S(1)} %sine_select_fusion), kind=kLoop, calls=%fused_computation.12 | loop fusion | flops 2359296 | bytes 9443328 | tf_op jit(solution)/shard_map/mul | solution.py:24
  13.6 12.8 %mul.213 = f32[256,9216]{1,0:T(8,128)} reshape(f32[16,16,96,96]{3,2,1,0:T(8,128)} %broadcast_multiply_fusion) | data formatting | bytes 18874368 | tf_op jit(solution)/shard_map/mul | solution.py:24
  26.4 11.1 %convolution_bitcast_fusion = f32[384,256]{0,1:T(8,128)S(1)} fusion(f32[256,9216]{1,0:T(8,128)} %mul.213, bf16[384,9216]{1,0:T(8,128)(2,1)} %bitcast.98), kind=kOutput, calls=%fused_computation.20 | convolution fusion | flops 10871635968 | bytes 16908288 | tf_op jit(solution)/shard_map/dot_general | solution.py:47
  37.5 0.2 copy.31
  37.7 0.4 fusion.16
  38.1 0.9 copy.32
  39.0 0.0 reduce-scatter.3.cloned.1.call-update
  39.0 0.0 reduce-scatter.5.cloned.1.call-start
  39.1 12.9 %reshape.211 = f32[256,9216,1]{1,0,2:T(8,128)} reshape(f32[16,16,96,96]{3,2,1,0:T(8,128)} %broadcast_multiply_fusion) | data formatting | bytes 18874368 | tf_op jit(solution)/shard_map/mul | solution.py:24
  52.0 0.0 copy-done
  52.0 11.8 %fusion.13 = f32[16,24,9216]{2,0,1:T(8,128)} fusion(bf16[16,24,9216]{2,1,0:T(8,128)(2,1)} %bitcast.99, bf16[16,16]{1,0:T(8,128)(2,1)S(1)} %copy-done), kind=kOutput, calls=%fused_computation.18 | convolution fusion | flops 113246208 | bytes 21234176 | tf_op jit(solution)/shard_map/sixz,io->soxz/dot_general | solution.py:71
  63.7 4.9 reduce-scatter.3.cloned.1.call-done
  68.6 0.0 copy-done.1
  68.6 1.1 multiply_reduce_fusion.1
  69.8 7.4 %all_gather.6 = f32[16,1,16,256]{3,2,1,0:T(8,128)S(1)} all-gather(f32[4,1,16,256]{3,2,1,0:T(8,128)S(1)} %bitcast.109), channel_id=1, replica_groups=mesh['dp'=32,'gz'=4] {'gz'}, dimensions={0}, use_global_device_ids=true | all-gather | bytes 327680 | tf_op jit(solution)/shard_map/all_gather | solution.py:68
  77.2 12.2 %fusion.24 = f32[16,16,9216]{2,0,1:T(8,128)S(1)} fusion(f32[256,9216,1]{1,0,2:T(8,128)} %reshape.211, f32[16,1,16,256]{3,2,1,0:T(8,128)S(1)} %all_gather.6), kind=kOutput, calls=%fused_computation.32 | convolution fusion | flops 7247757312 | bytes 19136512 | tf_op jit(solution)/shard_map/dot_general | solution.py:53
  89.4 0.0 slice-done.5
  89.4 0.0 slice-done.6
  89.4 0.0 copy-done.3
  89.4 0.0 slice-start.1
  89.4 0.0 slice-start.2
  89.5 25.9 %convert_reduce_fusion = (f32[16]{0:T(128)S(1)}, bf16[1,16,24,9216]{3,2,1,0:T(8,128)(2,1)}) fusion(f32[16]{0:T(128)S(1)} %copy-done.3, f32[16,24,9216]{2,0,1:T(8,128)} %fusion.13, f32[16,16,9216]{2,0,1:T(8,128)S(1)} %fusion.24, f32[16,96]{1,0:T(8,128)S(1)} %sine_select_fusion, s32[]{:T(128)S(6)} %select_n.65, bf16[1,16,24,9216]{3,2,1,0:T(8,128)(2,1)S(1)} %bitcast.112), kind=kOutput, calls=%fused_computation.11 | convolution fusion | flops 736100352 | bytes 37755012 | tf_op jit(solution)/shard_map/ax,asoz->soxz/dot_general | solution.py:57
  115.4 0.0 slice-done
  115.4 0.0 slice-done.1
  115.4 0.0 slice-done.2
  115.4 0.0 slice-start.4
  115.4 13.4 %fusion.47 = f32[16,24,256]{2,1,0:T(8,128)S(1)} fusion(f32[256,9216,1]{1,0,2:T(8,128)S(1)} %bitcast.97, bf16[1,16,24,9216]{3,2,1,0:T(8,128)(2,1)} %get-tuple-element.23), kind=kOutput, calls=%fused_computation.62 | convolution fusion | flops 10871635968 | bytes 16908288 | tf_op jit(solution)/shard_map/dot_general | solution.py:47
  128.9 17.8 %fusion.17 = f32[16,16]{0,1:T(8,128)S(1)} fusion(bf16[16,24,9216]{2,1,0:T(8,128)(2,1)S(1)} %bitcast.102, bf16[16,24,9216]{2,1,0:T(8,128)(2,1)} %bitcast.103), kind=kOutput, calls=%fused_computation.25 | convolution fusion | flops 113246208 | bytes 14156800 | tf_op jit(solution)/shard_map/sixz,soxz->io/dot_general | solution.py:89
  146.7 83.9 %all-reduce = (f32[16,16]{0,1:T(8,128)S(1)}, f32[16]{0:T(128)S(1)}) all-reduce(f32[16,16]{0,1:T(8,128)S(1)} %fusion.17, f32[16]{0:T(128)S(1)} %get-tuple-element.22), channel_id=1, replica_groups=mesh['dp'=32,'gz'=4] {'dp'}, use_global_device_ids=true, to_apply=%region_3.4 | all-reduce | flops 272 | bytes 2176 | tf_op jit(solution)/shard_map/psum | solution.py:91
  230.6 7.4 %all-reduce.1 = (f32[16,16]{0,1:T(8,128)S(1)}, f32[16]{0:T(128)S(1)}) all-reduce(f32[16,16]{0,1:T(8,128)S(1)} %get-tuple-element.16, f32[16]{0:T(128)S(1)} %get-tuple-element.17), channel_id=1, replica_groups=mesh['dp'=32,'gz'=4] {'gz'}, use_global_device_ids=true, to_apply=%region_4.5 | all-reduce | flops 272 | bytes 2176 | tf_op jit(solution)/shard_map/psum | solution.py:91
  238.0 0.7 copy.43
  238.7 0.5 broadcast_multiply_fusion.3
  239.2 0.4 fusion.15
  239.6 0.9 copy.37
  240.5 0.0 reduce-scatter.5.cloned.1.call-update
  240.5 0.0 all-reduce.4.cloned.1.call-start
  240.6 16.0 %fusion.10 = f32[24,9216,16]{1,2,0:T(8,128)} fusion(bf16[16,24,9216]{2,1,0:T(8,128)(2,1)} %bitcast.104, bf16[16,16]{1,0:T(8,128)(2,1)S(1)} %copy-done), kind=kOutput, calls=%fused_computation.15 | convolution fusion | flops 113246208 | bytes 21234176 | tf_op jit(solution)/shard_map/soxz,io->sixz/dot_general | solution.py:87
  256.6 6.4 %reduce-scatter.5.cloned.1.call-done = f32[4,1,16,256]{3,2,1,0:T(8,128)} async-done(((f32[16,1,16,256]{3,2,1,0:T(8,128)}), f32[4,1,16,256]{3,2,1,0:T(8,128)}) %reduce-scatter.5.cloned.1.call-update) | async-done | bytes 65552 | tf_op jit(solution)/shard_map/reduce_scatter | solution.py:77
  263.0 2.1 multiply_bitcast_fusion
  265.0 0.0 all-reduce.4.cloned.1.call-update
  265.1 7.3 %all_gather.7 = f32[16,1,16,256]{3,2,1,0:T(8,128)S(1)} all-gather(f32[4,1,16,256]{3,2,1,0:T(8,128)S(1)} %bitcast.108), channel_id=1, replica_groups=mesh['dp'=32,'gz'=4] {'gz'}, dimensions={0}, use_global_device_ids=true | all-gather | bytes 327680 | tf_op jit(solution)/shard_map/all_gather | solution.py:84
  272.4 12.2 %fusion.22 = f32[16,16,9216]{2,0,1:T(8,128)S(1)} fusion(f32[256,9216,1]{1,0,2:T(8,128)} %reshape.211, f32[16,1,16,256]{3,2,1,0:T(8,128)S(1)} %all_gather.7), kind=kOutput, calls=%fused_computation.30 | convolution fusion | flops 7247757312 | bytes 19136512 | tf_op jit(solution)/shard_map/dot_general | solution.py:53
  284.6 25.8 %fusion.6 = bf16[1,16,24,9216]{3,2,1,0:T(8,128)(2,1)} fusion(f32[24,9216,16]{1,2,0:T(8,128)} %fusion.10, f32[16,16,9216]{2,0,1:T(8,128)S(1)} %fusion.22, f32[16,96]{1,0:T(8,128)S(1)} %sine_select_fusion, s32[]{:T(128)S(6)} %select_n.65), kind=kOutput, calls=%fused_computation.8 | convolution fusion | flops 690094080 | bytes 30676996 | tf_op jit(solution)/shard_map/ax,asoz->soxz/dot_general | solution.py:57
  310.4 263.7 %all-reduce.4.cloned.1.call-done = f32[4,16,16,256]{3,2,1,0:T(8,128)} async-done(((f32[4,16,16,256]{3,2,1,0:T(8,128)}), f32[4,16,16,256]{3,2,1,0:T(8,128)}) %all-reduce.4.cloned.1.call-update) | async-done | bytes 1048592 | tf_op jit(solution)/shard_map/psum | solution.py:93
  574.1 2.3 broadcast_multiply_fusion.1
  (16 shorter events, 0.0 us)
Async XLA Ops:
  7.2 44.8 %copy-start = (bf16[16,16]{1,0:T(8,128)(2,1)S(1)}, bf16[16,16]{1,0:T(8,128)(2,1)}, u32[]{:S(2)}) copy-start(bf16[16,16]{1,0:T(8,128)(2,1)} %param.8) | copy-start | bytes 1540
  7.2 61.4 %reduce-scatter.3.cloned.1.call-start = ((), (), s32[]{:S(2)}) async-start(), calls=%async_computation.2 | async-start | bytes 327680 | tf_op jit(solution)/shard_map/reduce_scatter | solution.py:61
  39.0 224.0 %reduce-scatter.5.cloned.1.call-start = ((), (), s32[]{:S(2)}) async-start(), calls=%async_computation.3 | async-start | bytes 327680 | tf_op jit(solution)/shard_map/reduce_scatter | solution.py:77
  52.0 16.7 %copy-start.1 = (f32[4,16,16,256]{3,2,1,0:T(8,128)S(1)}, f32[4,16,16,256]{3,2,1,0:T(8,128)}, u32[]{:S(2)}) copy-start(f32[4,16,16,256]{3,2,1,0:T(8,128)} %param.7) | copy-start | bytes 3145732
  68.6 20.8 %slice-start.5 = ((s8[7077888]{0:T(1024)(128)(4,1)}), s8[4194304]{0:T(1024)(128)(4,1)S(1)}, s32[]{:S(2)}) async-start(s8[7077888]{0:T(1024)(128)(4,1)} %bitcast.111), calls=%async_computation.10 | async-start | bytes 8388608
  77.2 12.2 %slice-start.6 = ((s8[7077888]{0:T(1024)(128)(4,1)}), s8[2883584]{0:T(1024)(128)(4,1)S(1)}, s32[]{:S(2)}) async-start(s8[7077888]{0:T(1024)(128)(4,1)} %bitcast.111), calls=%async_computation.11 | async-start | bytes 5767168
  77.2 12.2 %copy-start.3 = (f32[16]{0:T(128)S(1)}, f32[16]{0:T(128)}, u32[]{:S(2)}) copy-start(f32[16]{0:T(128)} %param.9) | copy-start | bytes 196
  77.2 38.2 %slice-start = ((s8[9437184]{0:T(1024)(128)(4,1)}), s8[4194304]{0:T(1024)(128)(4,1)S(1)}, s32[]{:S(2)}) async-start(s8[9437184]{0:T(1024)(128)(4,1)} %bitcast.96), calls=%async_computation.5 | async-start | bytes 8388608
  89.4 26.0 %slice-start.1 = ((s8[9437184]{0:T(1024)(128)(4,1)}), s8[4194304]{0:T(1024)(128)(4,1)S(1)}, s32[]{:S(2)}) async-start(s8[9437184]{0:T(1024)(128)(4,1)} %bitcast.96), calls=%async_computation.6 | async-start | bytes 8388608
  89.4 26.0 %slice-start.2 = ((s8[9437184]{0:T(1024)(128)(4,1)}), s8[1048576]{0:T(1024)(128)(4,1)S(1)}, s32[]{:S(2)}) async-start(s8[9437184]{0:T(1024)(128)(4,1)} %bitcast.96), calls=%async_computation.7 | async-start | bytes 2097152
  115.4 13.5 %slice-start.3 = ((s8[7077888]{0:T(1024)(128)(4,1)}), s8[4194304]{0:T(1024)(128)(4,1)S(1)}, s32[]{:S(2)}) async-start(s8[7077888]{0:T(1024)(128)(4,1)} %bitcast.100), calls=%async_computation.8 | async-start | bytes 8388608
  115.4 13.4 %slice-start.4 = ((s8[7077888]{0:T(1024)(128)(4,1)}), s8[2883584]{0:T(1024)(128)(4,1)S(1)}, s32[]{:S(2)}) async-start(s8[7077888]{0:T(1024)(128)(4,1)} %bitcast.100), calls=%async_computation.9 | async-start | bytes 5767168
  240.5 22.5 %copy-start.2 = (f32[4,1,16,256]{3,2,1,0:T(8,128)S(1)}, f32[4,1,16,256]{3,2,1,0:T(8,128)}, u32[]{:S(2)}) copy-start(f32[4,1,16,256]{3,2,1,0:T(8,128)} %reduce-scatter.3.cloned.1.call-done) | copy-start | bytes 196612
  240.5 333.6 %all-reduce.4.cloned.1.call-start = ((), (), s32[]{:S(2)}) async-start(), calls=%async_computation.4 | async-start | bytes 2097152 | tf_op jit(solution)/shard_map/psum | solution.py:93
Sparse Core Ops, SparseCore 0:
  39.1 29.4 reduce-scatter.2
  240.6 22.2 reduce-scatter.4
  266.0 308.0 all-reduce.3
